TPU v7x, 256 devices: a whole 4x4x8 slice. The times are simulated.
256 devices in a mesh: adapter: 64 (over x, z, core), tensor: 4 (over y).
Axes of the slice: x: 4, y: 4, z: 8, core: 2. Of those that a mesh axis runs over, the one named last changes fastest.
Arguments:
- activations: bfloat16 [32768, 4096], P('adapter', 'tensor'), may hold values from -6 to 6
- output_gradient: bfloat16 [32768, 4096], P('adapter', 'tensor'), may hold values from -6 to 6
- frozen_weight: bfloat16 [4096, 4096], P(None, 'tensor'), may hold values from -0.09375 to 0.09375
- adapter_down_weight: bfloat16 [8192, 4096], P('adapter', 'tensor'), may hold values from -0.09375 to 0.09375
- adapter_up_weight: bfloat16 [8192, 4096], P('adapter', 'tensor'), may hold values from -0.09375 to 0.09375
- adapter_slot_table: int32 [512], replicated, may hold values from 0 to 511, as said below
- group_adapter_index: int32 [64, 48], P('adapter'), may hold values from 0 to 511, as said below
- group_token_length: int32 [64, 48], P('adapter'), may hold values from 1 to 16, as said below
Outputs:
- input_gradient: bfloat16 [32768, 4096], P('adapter', 'tensor')
- down_grad: float32 [8192, 4096], P('adapter', 'tensor')
- up_grad: float32 [8192, 4096], P('adapter', 'tensor')
Inputs may be any that keep to these rules, and one draw needn't show every extreme that they name: `adapter_slot_table`: a permutation of the slots; slot k lies on adapter index k // 8. `group_adapter_index`: the adapters of one index's groups lie on distinct indices of the adapter axis; on every index one group of exactly 16 tokens uses an adapter stored on one index that is the same for all indices. `group_token_length`: each row sums to 512 and holds a group of exactly 16 tokens.
All inputs are finite; a program needn't handle non-finite values.
Results may differ from a plain program's by a relative error of at most 0.015.
Values may be sent and summed in bfloat16 or wider, within the bound.
A program may use at most 128 MiB of HBM per device.

v0:
```python
import jax
import jax.numpy as jnp
from jax import lax
from jax.sharding import PartitionSpec as P

ADAPTER_RANK = 16
ADP_DEV = 8
adapter_scale = 2.0


def rank_sums(down_part, up_part):
    return (
        lax.psum(down_part.astype(jnp.bfloat16), "tensor").astype(jnp.float32),
        lax.psum(up_part.astype(jnp.bfloat16), "tensor").astype(jnp.float32),
    )


def widen(mask, values):
    return jnp.where(mask[:, :, None], values[:, None, :], jnp.zeros((), values.dtype)).reshape(
        values.shape[0], mask.shape[1] * values.shape[1]
    )


def narrow(wide, mask):
    shaped = wide.reshape(wide.shape[0], mask.shape[1], ADAPTER_RANK)
    return jnp.sum(shaped * mask[:, :, None].astype(jnp.float32), axis=1)


def on_device(
    activations,
    output_gradient,
    frozen_weight,
    adapter_down_weight,
    adapter_up_weight,
    adapter_slot_table,
    group_adapter_index,
    group_token_length,
):
    tok_rows = activations.shape[0]
    devices = lax.axis_size("adapter")
    own_index = lax.axis_index("adapter")
    adapter_count = adapter_slot_table.shape[0]
    lengths = group_token_length[0]
    matched = group_adapter_index[0][:, None] == jnp.arange(adapter_count, dtype=jnp.int32)[None, :]
    group_slot = jnp.sum(jnp.where(matched, adapter_slot_table[None, :], 0), axis=1)
    group_owner = group_slot // ADP_DEV
    group_end = jnp.cumsum(lengths)
    positions = jnp.arange(tok_rows, dtype=jnp.int32)
    tok_group = jnp.sum((positions[:, None] >= group_end[None, :]).astype(jnp.int32), axis=1)
    group_onehot = tok_group[:, None] == jnp.arange(lengths.shape[0], dtype=jnp.int32)[None, :]
    tok_owner = jnp.sum(jnp.where(group_onehot, group_owner[None, :], 0), axis=1)
    gathered = lax.all_gather(jnp.stack([group_slot, lengths])[None], "adapter", axis=0, tiled=True)
    from_mine = gathered[:, 0] // ADP_DEV == own_index
    source_count = jnp.sum(jnp.where(from_mine, gathered[:, 1], 0), axis=1)
    source_local = jnp.sum(jnp.where(from_mine, gathered[:, 0] % ADP_DEV, 0), axis=1)
    source_hot = (source_local[:, None] == jnp.arange(ADP_DEV, dtype=jnp.int32)[None, :]) & (
        source_count > 0
    )[:, None]
    eye_rank = jnp.eye(ADAPTER_RANK, dtype=bool)
    selector = (source_hot[:, None, :, None] & eye_rank[None, :, None, :]).reshape(
        devices * ADAPTER_RANK, ADP_DEV * ADAPTER_RANK
    )
    selected_reduced = selector.astype(jnp.bfloat16)
    outgoing_down = jnp.dot(
        selected_reduced, adapter_down_weight, preferred_element_type=jnp.float32
    ).astype(jnp.bfloat16)
    outgoing_up = jnp.dot(
        selected_reduced, adapter_up_weight, preferred_element_type=jnp.float32
    ).astype(jnp.bfloat16)
    received_down, got_up = (
        lax.all_to_all(outgoing_down, "adapter", split_axis=0, concat_axis=0, tiled=True),
        lax.all_to_all(outgoing_up, "adapter", split_axis=0, concat_axis=0, tiled=True),
    )
    owner_hot = tok_owner[:, None] == jnp.arange(devices, dtype=jnp.int32)[None, :]
    down_wide = lax.dot_general(
        activations, received_down, (((1,), (1,)), ((), ())), preferred_element_type=jnp.float32
    )
    up_wide = lax.dot_general(
        output_gradient, got_up, (((1,), (1,)), ((), ())), preferred_element_type=jnp.float32
    )
    down_proj, up_proj = rank_sums(narrow(down_wide, owner_hot), narrow(up_wide, owner_hot))
    down_spread = widen(owner_hot, down_proj.astype(jnp.bfloat16))
    up_broadcast = widen(owner_hot, up_proj.astype(jnp.bfloat16))
    adapter_term = (
        adapter_scale * jnp.dot(up_broadcast, received_down, preferred_element_type=jnp.float32)
    ).astype(jnp.bfloat16)
    partial_down = adapter_scale * lax.dot_general(
        up_broadcast, activations, (((0,), (0,)), ((), ())), preferred_element_type=jnp.float32
    )
    partial_up = adapter_scale * lax.dot_general(
        down_spread, output_gradient, (((0,), (0,)), ((), ())), preferred_element_type=jnp.float32
    )
    back_down, back_up = (
        lax.all_to_all(
            partial_down.astype(jnp.bfloat16), "adapter", split_axis=0, concat_axis=0, tiled=True
        ).astype(partial_down.dtype),
        lax.all_to_all(
            partial_up.astype(jnp.bfloat16), "adapter", split_axis=0, concat_axis=0, tiled=True
        ).astype(partial_up.dtype),
    )
    select_full = selector.astype(jnp.float32)
    down_grad = lax.dot_general(
        select_full,
        back_down,
        (((0,), (0,)), ((), ())),
        precision=lax.Precision.HIGHEST,
        preferred_element_type=jnp.float32,
    )
    up_grad = lax.dot_general(
        select_full,
        back_up,
        (((0,), (0,)), ((), ())),
        precision=lax.Precision.HIGHEST,
        preferred_element_type=jnp.float32,
    )
    frozen_total_sum = lax.psum_scatter(
        lax.dot_general(
            frozen_weight,
            output_gradient,
            (((1,), (1,)), ((), ())),
            preferred_element_type=jnp.float32,
        ).astype(jnp.bfloat16),
        "tensor",
        scatter_dimension=0,
        tiled=True,
    ).astype(jnp.float32)
    input_gradient = (frozen_total_sum.T + adapter_term.astype(jnp.float32)).astype(jnp.bfloat16)
    return (input_gradient, down_grad, up_grad)


def solution(mesh):
    in_specs = (
        P("adapter", "tensor"),
        P("adapter", "tensor"),
        P(None, "tensor"),
        P("adapter", "tensor"),
        P("adapter", "tensor"),
        P(),
        P("adapter", None),
        P("adapter", None),
    )
    out_specs = (P("adapter", "tensor"), P("adapter", "tensor"), P("adapter", "tensor"))
    return jax.shard_map(
        on_device, mesh=mesh, in_specs=in_specs, out_specs=out_specs, check_vma=False
    )
```

profile of v0, /device:TPU:1, one launch (start us, length us, event | category | flops | bytes accessed | tf_op | source)
XLA Modules:
  0.0 331.1 jit_solution(9683461043637806220)
XLA Ops:
  7.2 0.0 copy-start
  7.2 0.0 copy-start.4
  7.2 1.0 select_reduce_fusion.1
  8.2 0.7 add_bitcast_fusion
  8.8 48.1 %all-gather.1 = s32[64,2,48]{2,1,0:T(2,128)S(1)} all-gather(s32[1,2,48]{2,1,0:T(2,128)S(1)} %add_bitcast_fusion), channel_id=2, replica_groups=mesh['adapter'=64,'tensor'=4] {'adapter'}, dimensions={0}, use_global_device_ids=true | all-gather | bytes 24960 | tf_op jit(solution)/shard_map/all_gather | solution.py:52
  57.0 0.1 fusion.10
  57.1 0.1 select_reduce_fusion.2
  57.2 0.1 fusion.6
  57.3 0.5 broadcast_and_fusion
  57.8 1.5 and.72
  59.3 0.0 copy-done.4
  59.3 2.0 convolution_convert_fusion.1
  61.3 0.0 copy-start.5
  61.3 6.6 %all-to-all-start.1 = ((bf16[64,16,1024]{2,1,0:T(8,128)(2,1)}), bf16[64,16,1024]{2,1,0:T(8,128)(2,1)S(1)}, u32[]{:S(2)}, u32[]{:S(2)}) async-start(bf16[64,16,1024]{2,1,0:T(8,128)(2,1)} %bitcast.11), calls=%async_computation.2 | async-start | bytes 4194304 | tf_op jit(solution)/shard_map/all_to_all | solution.py:71
  67.9 0.0 copy-done.5
  67.9 2.0 convolution_convert_fusion.2
  70.0 49.2 %all-to-all-done.1 = bf16[64,16,1024]{2,1,0:T(8,128)(2,1)S(1)} async-done(((bf16[64,16,1024]{2,1,0:T(8,128)(2,1)}), bf16[64,16,1024]{2,1,0:T(8,128)(2,1)S(1)}, u32[]{:S(2)}, u32[]{:S(2)}) %all-to-all-start.1) | async-done | bytes 2097184 | tf_op jit(solution)/shard_map/all_to_all | solution.py:71
  119.2 0.0 copy-start.1
  119.2 6.1 %all-to-all-start = ((bf16[64,16,1024]{2,1,0:T(8,128)(2,1)}), bf16[64,16,1024]{2,1,0:T(8,128)(2,1)}, u32[]{:S(2)}, u32[]{:S(2)}) async-start(bf16[64,16,1024]{2,1,0:T(8,128)(2,1)} %bitcast.7), calls=%async_computation.1 | async-start | bytes 4194304 | tf_op jit(solution)/shard_map/all_to_all | solution.py:72
  125.3 0.0 copy-done.6
  125.3 0.1 copy.27
  125.4 0.1 reduce-window.8
  125.5 0.1 reduce
  125.6 0.1 convert_reduce_fusion
  125.7 0.1 select_reduce_fusion
  125.9 0.0 copy-done.1
  125.9 3.9 %fusion.13 = f32[1024,512]{1,0:T(8,128)} fusion(bf16[1024,1024]{1,0:T(8,128)(2,1)S(1)} %bitcast.57, bf16[512,1024]{1,0:T(8,128)(2,1)} %param.8), kind=kOutput, calls=%fused_computation.47 | convolution fusion | flops 1073741824 | bytes 5242880 | tf_op jit(solution)/shard_map/dot_general | solution.py:75
  129.7 46.8 %all-to-all-done = bf16[64,16,1024]{2,1,0:T(8,128)(2,1)} async-done(((bf16[64,16,1024]{2,1,0:T(8,128)(2,1)}), bf16[64,16,1024]{2,1,0:T(8,128)(2,1)}, u32[]{:S(2)}, u32[]{:S(2)}) %all-to-all-start) | async-done | bytes 2097184 | tf_op jit(solution)/shard_map/all_to_all | solution.py:72
  176.5 0.0 copy-done
  176.5 3.0 fusion.11
  179.5 0.0 copy-done.3
  179.5 0.7 multiply_reduce_fusion
  180.2 13.6 %all-reduce = (bf16[512,16]{0,1:T(8,128)(2,1)S(1)}, bf16[512,16]{0,1:T(8,128)(2,1)S(1)}) all-reduce(bf16[512,16]{0,1:T(8,128)(2,1)S(1)} %get-tuple-element.16, bf16[512,16]{0,1:T(8,128)(2,1)S(1)} %get-tuple-element.15), channel_id=1, replica_groups=mesh['adapter'=64,'tensor'=4] {'tensor'}, use_global_device_ids=true, to_apply=%region_8.9 | all-reduce | flops 16384 | bytes 65536 | tf_op jit(solution)/shard_map/psum | solution.py:14
  193.8 1.2 broadcast_select_fusion
  195.0 2.6 multiply_convert_fusion
  197.6 9.6 %all-to-all-start.3 = ((bf16[64,16,1024]{2,1,0:T(8,128)(2,1)}), bf16[64,16,1024]{2,1,0:T(8,128)(2,1)S(1)}, u32[]{:S(2)}, u32[]{:S(2)}) async-start(bf16[64,16,1024]{2,1,0:T(8,128)(2,1)} %bitcast.58), calls=%async_computation.4 | async-start | bytes 4194304 | tf_op jit(solution)/shard_map/all_to_all | solution.py:97
  207.2 0.2 reduce-scatter.2.cloned.1.call-start
  207.4 9.6 %convolution_convert_fusion = bf16[4096,512]{1,0:T(8,128)(2,1)} fusion(bf16[4096,1024]{1,0:T(8,128)(2,1)} %param.10, bf16[512,1024]{1,0:T(8,128)(2,1)S(1)} %copy-done), kind=kOutput, calls=%fused_computation | convolution fusion | flops 4297064448 | bytes 13631488 | tf_op jit(solution)/shard_map/dot_general | solution.py:117
  217.0 0.0 reduce-scatter.2.cloned.1.call-update
  217.0 4.2 %multiply_convert_fusion.1 = bf16[1024,1024]{1,0:T(8,128)(2,1)} fusion(bf16[512,1024]{0,1:T(8,128)(2,1)} %bitcast.62, bf16[512,1024]{1,0:T(8,128)(2,1)} %param.8), kind=kOutput, calls=%fused_computation.2 | convolution fusion | flops 1075838976 | bytes 4194304 | tf_op jit(solution)/shard_map/dot_general | solution.py:87
  221.2 37.2 %all-to-all-done.3 = bf16[64,16,1024]{2,1,0:T(8,128)(2,1)S(1)} async-done(((bf16[64,16,1024]{2,1,0:T(8,128)(2,1)}), bf16[64,16,1024]{2,1,0:T(8,128)(2,1)S(1)}, u32[]{:S(2)}, u32[]{:S(2)}) %all-to-all-start.3) | async-done | bytes 2097184 | tf_op jit(solution)/shard_map/all_to_all | solution.py:97
  258.4 6.0 %all-to-all-start.2 = ((bf16[64,16,1024]{2,1,0:T(8,128)(2,1)}), bf16[64,16,1024]{2,1,0:T(8,128)(2,1)}, u32[]{:S(2)}, u32[]{:S(2)}) async-start(bf16[64,16,1024]{2,1,0:T(8,128)(2,1)} %bitcast.59), calls=%async_computation.3 | async-start | bytes 4194304 | tf_op jit(solution)/shard_map/all_to_all | solution.py:94
  264.4 1.3 fusion.14
  265.7 49.9 %all-to-all-done.2 = bf16[64,16,1024]{2,1,0:T(8,128)(2,1)} async-done(((bf16[64,16,1024]{2,1,0:T(8,128)(2,1)}), bf16[64,16,1024]{2,1,0:T(8,128)(2,1)}, u32[]{:S(2)}, u32[]{:S(2)}) %all-to-all-start.2) | async-done | bytes 2097184 | tf_op jit(solution)/shard_map/all_to_all | solution.py:94
  315.6 2.9 fusion.12
  318.5 0.0 copy-done.2
  318.5 3.5 %fusion.1 = bf16[512,1024]{0,1:T(8,128)(2,1)} fusion(bf16[1024,512]{1,0:T(8,128)(2,1)} %reduce-scatter.2.cloned.1.call-done, bf16[64,16,1024]{2,1,0:T(8,128)(2,1)S(1)} %copy-done.2, pred[512,64]{0,1:T(8,128)(4,1)S(1)} %get-tuple-element.26, bf16[512,16]{0,1:T(8,128)(2,1)S(1)} %get-tuple-element.19), kind=kOutput, calls=%fused_computation.6 | convolution fusion | flops 1077411840 | bytes 4243456 | tf_op jit(solution)/shard_map/dot_general | solution.py:85
  322.0 2.3 copy.30
  (8 shorter events, 0.1 us)
Async XLA Ops:
  7.2 169.3 %copy-start = (bf16[512,1024]{1,0:T(8,128)(2,1)S(1)}, bf16[512,1024]{1,0:T(8,128)(2,1)}, u32[]{:S(2)}) copy-start(bf16[512,1024]{1,0:T(8,128)(2,1)} %param.9) | copy-start | bytes 3145732
  7.2 52.1 %copy-start.4 = (bf16[128,1024]{1,0:T(8,128)(2,1)S(1)}, bf16[128,1024]{1,0:T(8,128)(2,1)}, u32[]{:S(2)}) copy-start(bf16[128,1024]{1,0:T(8,128)(2,1)} %param.11) | copy-start | bytes 786436
  61.3 6.6 %copy-start.5 = (bf16[128,1024]{1,0:T(8,128)(2,1)S(1)}, bf16[128,1024]{1,0:T(8,128)(2,1)}, u32[]{:S(2)}) copy-start(bf16[128,1024]{1,0:T(8,128)(2,1)} %param.12) | copy-start | bytes 786436
  61.3 57.8 %all-to-all-start.1 = ((bf16[64,16,1024]{2,1,0:T(8,128)(2,1)}), bf16[64,16,1024]{2,1,0:T(8,128)(2,1)S(1)}, u32[]{:S(2)}, u32[]{:S(2)}) async-start(bf16[64,16,1024]{2,1,0:T(8,128)(2,1)} %bitcast.11), calls=%async_computation.2 | async-start | bytes 4194304 | tf_op jit(solution)/shard_map/all_to_all | solution.py:71
  119.2 6.7 %copy-start.1 = (bf16[64,16,1024]{2,1,0:T(8,128)(2,1)}, bf16[64,16,1024]{2,1,0:T(8,128)(2,1)S(1)}, u32[]{:S(2)}) copy-start(bf16[64,16,1024]{2,1,0:T(8,128)(2,1)S(1)} %all-to-all-done.1) | copy-start | bytes 6291460
  119.2 6.1 %copy-start.6 = (s32[1,48]{1,0:T(1,128)S(1)}, s32[1,48]{1,0:T(1,128)}, u32[]{:S(2)}) copy-start(s32[1,48]{1,0:T(1,128)} %param.15) | copy-start | bytes 580
  119.2 57.3 %all-to-all-start = ((bf16[64,16,1024]{2,1,0:T(8,128)(2,1)}), bf16[64,16,1024]{2,1,0:T(8,128)(2,1)}, u32[]{:S(2)}, u32[]{:S(2)}) async-start(bf16[64,16,1024]{2,1,0:T(8,128)(2,1)} %bitcast.7), calls=%async_computation.1 | async-start | bytes 4194304 | tf_op jit(solution)/shard_map/all_to_all | solution.py:72
  176.5 3.0 copy-start.3
  197.6 60.8 %all-to-all-start.3 = ((bf16[64,16,1024]{2,1,0:T(8,128)(2,1)}), bf16[64,16,1024]{2,1,0:T(8,128)(2,1)S(1)}, u32[]{:S(2)}, u32[]{:S(2)}) async-start(bf16[64,16,1024]{2,1,0:T(8,128)(2,1)} %bitcast.58), calls=%async_computation.4 | async-start | bytes 4194304 | tf_op jit(solution)/shard_map/all_to_all | solution.py:97
  207.2 111.3 %reduce-scatter.2.cloned.1.call-start = ((), (), s32[]{:S(2)}) async-start(), calls=%async_computation.5 | async-start | bytes 5242880 | tf_op jit(solution)/shard_map/reduce_scatter | solution.py:116
  258.4 57.2 %all-to-all-start.2 = ((bf16[64,16,1024]{2,1,0:T(8,128)(2,1)}), bf16[64,16,1024]{2,1,0:T(8,128)(2,1)}, u32[]{:S(2)}, u32[]{:S(2)}) async-start(bf16[64,16,1024]{2,1,0:T(8,128)(2,1)} %bitcast.59), calls=%async_computation.3 | async-start | bytes 4194304 | tf_op jit(solution)/shard_map/all_to_all | solution.py:94
  265.7 52.8 %copy-start.2 = (bf16[64,16,1024]{2,1,0:T(8,128)(2,1)S(1)}, bf16[64,16,1024]{2,1,0:T(8,128)(2,1)}, u32[]{:S(2)}) copy-start(bf16[64,16,1024]{2,1,0:T(8,128)(2,1)} %copy-done.1) | copy-start | bytes 6291460
Sparse Core Ops, SparseCore 0:
  217.1 48.8 reduce-scatter.1
where the time goes:
time: 332 us; the launch traced here: 331 us
  waiting for transfers between devices  183 us (55%)
  blocking collectives  61.7 us (19%)
  matrix products  35 us (11%)
  starting transfers between devices  28.5 us (9%)
  between operations  14.2 us (4%)
  other arithmetic  4.68 us (1%)
  local copies, waits for them, and re-layouts  3.91 us (1%)
    all_to_all x1, waiting for transfers between devices, on_device(): lax.all_to_all(partial_down.astype(jnp.bfloat16), 'adapter', split_axis=0...  49.9 us
    all_to_all x1, waiting for transfers between devices, on_device(): lax.all_to_all(outgoing_down, 'adapter', split_axis=0, concat_axis=0, til...  49.2 us
    all_gather x1, blocking collectives, on_device(): lax.all_gather(jnp.stack([group_slot, lengths])[None], 'adapter', axis=0,...  48.1 us
    all_to_all x1, waiting for transfers between devices, on_device(): lax.all_to_all(outgoing_up, 'adapter', split_axis=0, concat_axis=0, tiled...  46.8 us
    all_to_all x1, waiting for transfers between devices, on_device(): lax.all_to_all(partial_up.astype(jnp.bfloat16), 'adapter', split_axis=0,...  37.2 us
    psum x1, blocking collectives, rank_sums(): lax.psum(up_part.astype(jnp.bfloat16), 'tensor').astype(jnp.float32)  13.6 us
    all_to_all x1, starting transfers between devices, on_device(): lax.all_to_all(partial_up.astype(jnp.bfloat16), 'adapter', split_axis=0,...  9.57 us
    dot_general x1, matrix products, on_device(): lax.dot_general(frozen_weight, output_gradient, (((1,), (1,)), ((), ())),...  9.56 us
  transfers between devices with their start and end apart: 5, of which 4 were waited for; matrix products, arithmetic and copies ran while one was open for 7% of the time, Pallas kernels for 0%

commit v1 on v0

--- a/solution.py
+++ b/solution.py
@@ -49,7 +49,15 @@
     tok_group = jnp.sum((positions[:, None] >= group_end[None, :]).astype(jnp.int32), axis=1)
     group_onehot = tok_group[:, None] == jnp.arange(lengths.shape[0], dtype=jnp.int32)[None, :]
     tok_owner = jnp.sum(jnp.where(group_onehot, group_owner[None, :], 0), axis=1)
-    gathered = lax.all_gather(jnp.stack([group_slot, lengths])[None], "adapter", axis=0, tiled=True)
+    gathered = jnp.concatenate(
+        lax.all_to_all(
+            jnp.stack([jnp.stack([group_slot, lengths])[None]] * lax.axis_size("adapter")),
+            "adapter",
+            0,
+            0,
+        ),
+        axis=0,
+    )
     from_mine = gathered[:, 0] // ADP_DEV == own_index
     source_count = jnp.sum(jnp.where(from_mine, gathered[:, 1], 0), axis=1)
     source_local = jnp.sum(jnp.where(from_mine, gathered[:, 0] % ADP_DEV, 0), axis=1)

time: 332 us -> 305 us (0.919)
  blocking collectives: 61.7 us -> 13.6 us
  starting transfers between devices: 28.5 us -> 39.6 us
  waiting for transfers between devices: 183 us -> 193 us
    all_gather x1 -> x0, blocking collectives: 48.1 us -> none  [on_device(): lax.all_gather(jnp.stack([group_slot, lengths])[None], 'adapter', axis=0,...]
    all_to_all x0 -> x1, starting transfers between devices: none -> 13 us  [on_device(): lax.all_to_all(jnp.stack([jnp.stack([group_slot, lengths])[None]] * lax.a...]
    all_to_all x0 -> x1, waiting for transfers between devices: none -> 9.77 us  [on_device(): lax.all_to_all(jnp.stack([jnp.stack([group_slot, lengths])[None]] * lax.a...]
  transfers between devices with their start and end apart: 5 -> 6, of which waited for: 4 -> 5; matrix products, arithmetic and copies ran while one was open for 7% -> 8% of each run, Pallas kernels for 0% -> 0%
where the time goes in v1:
time: 305 us
  waiting for transfers between devices  193 us (63%)
  starting transfers between devices  39.6 us (13%)
  matrix products  35 us (11%)
  between operations  14.2 us (5%)
  blocking collectives  13.6 us (4%)
  other arithmetic  4.68 us (2%)
  local copies, waits for them, and re-layouts  4.56 us (1%)
    all_to_all x1, waiting for transfers between devices, on_device(): lax.all_to_all(partial_down.astype(jnp.bfloat16), 'adapter', split_axis=0...  49.9 us
    all_to_all x1, waiting for transfers between devices, on_device(): lax.all_to_all(outgoing_down, 'adapter', split_axis=0, concat_axis=0, til...  49.3 us
    all_to_all x1, waiting for transfers between devices, on_device(): lax.all_to_all(outgoing_up, 'adapter', split_axis=0, concat_axis=0, tiled...  46.8 us
    all_to_all x1, waiting for transfers between devices, on_device(): lax.all_to_all(partial_up.astype(jnp.bfloat16), 'adapter', split_axis=0,...  37.2 us
    psum x1, blocking collectives, rank_sums(): lax.psum(up_part.astype(jnp.bfloat16), 'tensor').astype(jnp.float32)  13.6 us
    all_to_all x1, starting transfers between devices, on_device(): lax.all_to_all(jnp.stack([jnp.stack([group_slot, lengths])[None]] * lax.a...  13 us
    all_to_all x1, waiting for transfers between devices, on_device(): lax.all_to_all(jnp.stack([jnp.stack([group_slot, lengths])[None]] * lax.a...  9.77 us
    all_to_all x1, starting transfers between devices, on_device(): lax.all_to_all(partial_up.astype(jnp.bfloat16), 'adapter', split_axis=0,...  9.57 us
  transfers between devices with their start and end apart: 6, of which 5 were waited for; matrix products, arithmetic and copies ran while one was open for 8% of the time, Pallas kernels for 0%

profile of v1, /device:TPU:1, one launch (start us, length us, event | category | flops | bytes accessed | tf_op | source)
XLA Modules:
  0.0 304.6 jit_solution(9300123994571639739)
XLA Ops:
  7.2 0.0 copy-start
  7.2 0.0 copy-start.4
  7.2 1.0 select_reduce_fusion.1
  8.2 0.7 pad_add_fusion
  8.8 0.6 stack.8
  9.5 13.0 %all-to-all-start = ((s32[64,1,2,48]{3,2,1,0:T(2,128)}), s32[64,1,2,48]{3,2,1,0:T(2,128)S(1)}, u32[]{:S(2)}, u32[]{:S(2)}) async-start(s32[64,1,2,48]{3,2,1,0:T(2,128)} %stack.8), calls=%async_computation.1 | async-start | bytes 131072 | tf_op jit(solution)/shard_map/all_to_all | solution.py:53
  22.5 9.8 %all-to-all-done = s32[64,1,2,48]{3,2,1,0:T(2,128)S(1)} async-done(((s32[64,1,2,48]{3,2,1,0:T(2,128)}), s32[64,1,2,48]{3,2,1,0:T(2,128)S(1)}, u32[]{:S(2)}, u32[]{:S(2)}) %all-to-all-start) | async-done | bytes 24608 | tf_op jit(solution)/shard_map/all_to_all | solution.py:53
  32.3 0.1 fusion.10
  32.3 0.1 select_reduce_fusion.2
  32.5 0.1 fusion.6
  32.6 0.5 broadcast_and_fusion
  33.1 1.5 and.72
  34.6 0.0 copy-done.4
  34.6 2.0 convolution_convert_fusion.1
  36.6 4.7 %all-to-all-start.2 = ((bf16[64,16,1024]{2,1,0:T(8,128)(2,1)}), bf16[64,16,1024]{2,1,0:T(8,128)(2,1)S(1)}, u32[]{:S(2)}, u32[]{:S(2)}) async-start(bf16[64,16,1024]{2,1,0:T(8,128)(2,1)} %bitcast.11), calls=%async_computation.3 | async-start | bytes 4194304 | tf_op jit(solution)/shard_map/all_to_all | solution.py:79
  41.2 0.0 copy-done.5
  41.3 2.0 convolution_convert_fusion.2
  43.3 49.3 %all-to-all-done.2 = bf16[64,16,1024]{2,1,0:T(8,128)(2,1)S(1)} async-done(((bf16[64,16,1024]{2,1,0:T(8,128)(2,1)}), bf16[64,16,1024]{2,1,0:T(8,128)(2,1)S(1)}, u32[]{:S(2)}, u32[]{:S(2)}) %all-to-all-start.2) | async-done | bytes 2097184 | tf_op jit(solution)/shard_map/all_to_all | solution.py:79
  92.6 6.1 %all-to-all-start.1 = ((bf16[64,16,1024]{2,1,0:T(8,128)(2,1)}), bf16[64,16,1024]{2,1,0:T(8,128)(2,1)}, u32[]{:S(2)}, u32[]{:S(2)}) async-start(bf16[64,16,1024]{2,1,0:T(8,128)(2,1)} %bitcast.7), calls=%async_computation.2 | async-start | bytes 4194304 | tf_op jit(solution)/shard_map/all_to_all | solution.py:80
  98.8 0.0 copy-done.6
  98.8 0.1 copy.30
  98.9 0.1 reduce-window.8
  98.9 0.1 reduce
  99.0 0.1 convert_reduce_fusion
  99.2 0.1 select_reduce_fusion
  99.3 0.0 copy-done.1
  99.3 3.9 %fusion.13 = f32[1024,512]{1,0:T(8,128)} fusion(bf16[1024,1024]{1,0:T(8,128)(2,1)S(1)} %bitcast.56, bf16[512,1024]{1,0:T(8,128)(2,1)} %param.8), kind=kOutput, calls=%fused_computation.47 | convolution fusion | flops 1073741824 | bytes 5242880 | tf_op jit(solution)/shard_map/dot_general | solution.py:83
  103.2 46.8 %all-to-all-done.1 = bf16[64,16,1024]{2,1,0:T(8,128)(2,1)} async-done(((bf16[64,16,1024]{2,1,0:T(8,128)(2,1)}), bf16[64,16,1024]{2,1,0:T(8,128)(2,1)}, u32[]{:S(2)}, u32[]{:S(2)}) %all-to-all-start.1) | async-done | bytes 2097184 | tf_op jit(solution)/shard_map/all_to_all | solution.py:80
  149.9 0.0 copy-done
  149.9 3.0 fusion.11
  152.9 0.0 copy-done.3
  153.0 0.7 multiply_reduce_fusion
  153.6 13.6 %all-reduce = (bf16[512,16]{0,1:T(8,128)(2,1)S(1)}, bf16[512,16]{0,1:T(8,128)(2,1)S(1)}) all-reduce(bf16[512,16]{0,1:T(8,128)(2,1)S(1)} %get-tuple-element.19, bf16[512,16]{0,1:T(8,128)(2,1)S(1)} %get-tuple-element.18), channel_id=1, replica_groups=mesh['adapter'=64,'tensor'=4] {'tensor'}, use_global_device_ids=true, to_apply=%region_8.9 | all-reduce | flops 16384 | bytes 65536 | tf_op jit(solution)/shard_map/psum | solution.py:14
  167.2 1.2 broadcast_select_fusion
  168.4 2.6 multiply_convert_fusion
  171.0 9.6 %all-to-all-start.4 = ((bf16[64,16,1024]{2,1,0:T(8,128)(2,1)}), bf16[64,16,1024]{2,1,0:T(8,128)(2,1)S(1)}, u32[]{:S(2)}, u32[]{:S(2)}) async-start(bf16[64,16,1024]{2,1,0:T(8,128)(2,1)} %bitcast.57), calls=%async_computation.5 | async-start | bytes 4194304 | tf_op jit(solution)/shard_map/all_to_all | solution.py:105
  180.6 0.2 reduce-scatter.2.cloned.1.call-start
  180.8 9.6 %convolution_convert_fusion = bf16[4096,512]{1,0:T(8,128)(2,1)} fusion(bf16[4096,1024]{1,0:T(8,128)(2,1)} %param.10, bf16[512,1024]{1,0:T(8,128)(2,1)S(1)} %copy-done), kind=kOutput, calls=%fused_computation | convolution fusion | flops 4297064448 | bytes 13631488 | tf_op jit(solution)/shard_map/dot_general | solution.py:125
  190.4 0.0 reduce-scatter.2.cloned.1.call-update
  190.4 4.2 %multiply_convert_fusion.1 = bf16[1024,1024]{1,0:T(8,128)(2,1)} fusion(bf16[512,1024]{0,1:T(8,128)(2,1)} %bitcast.61, bf16[512,1024]{1,0:T(8,128)(2,1)} %param.8), kind=kOutput, calls=%fused_computation.2 | convolution fusion | flops 1075838976 | bytes 4194304 | tf_op jit(solution)/shard_map/dot_general | solution.py:95
  194.6 37.2 %all-to-all-done.4 = bf16[64,16,1024]{2,1,0:T(8,128)(2,1)S(1)} async-done(((bf16[64,16,1024]{2,1,0:T(8,128)(2,1)}), bf16[64,16,1024]{2,1,0:T(8,128)(2,1)S(1)}, u32[]{:S(2)}, u32[]{:S(2)}) %all-to-all-start.4) | async-done | bytes 2097184 | tf_op jit(solution)/shard_map/all_to_all | solution.py:105
  231.8 6.0 %all-to-all-start.3 = ((bf16[64,16,1024]{2,1,0:T(8,128)(2,1)}), bf16[64,16,1024]{2,1,0:T(8,128)(2,1)}, u32[]{:S(2)}, u32[]{:S(2)}) async-start(bf16[64,16,1024]{2,1,0:T(8,128)(2,1)} %bitcast.58), calls=%async_computation.4 | async-start | bytes 4194304 | tf_op jit(solution)/shard_map/all_to_all | solution.py:102
  237.9 1.3 fusion.14
  239.2 49.9 %all-to-all-done.3 = bf16[64,16,1024]{2,1,0:T(8,128)(2,1)} async-done(((bf16[64,16,1024]{2,1,0:T(8,128)(2,1)}), bf16[64,16,1024]{2,1,0:T(8,128)(2,1)}, u32[]{:S(2)}, u32[]{:S(2)}) %all-to-all-start.3) | async-done | bytes 2097184 | tf_op jit(solution)/shard_map/all_to_all | solution.py:102
  289.0 2.9 fusion.12
  291.9 0.0 copy-done.2
  291.9 3.5 %fusion.1 = bf16[512,1024]{0,1:T(8,128)(2,1)} fusion(bf16[1024,512]{1,0:T(8,128)(2,1)} %reduce-scatter.2.cloned.1.call-done, bf16[64,16,1024]{2,1,0:T(8,128)(2,1)S(1)} %copy-done.2, pred[512,64]{0,1:T(8,128)(4,1)S(1)} %get-tuple-element.29, bf16[512,16]{0,1:T(8,128)(2,1)S(1)} %get-tuple-element.22), kind=kOutput, calls=%fused_computation.6 | convolution fusion | flops 1077411840 | bytes 4243456 | tf_op jit(solution)/shard_map/dot_general | solution.py:93
  295.4 2.3 copy.35
  (10 shorter events, 0.1 us)
Async XLA Ops:
  7.2 142.8 %copy-start = (bf16[512,1024]{1,0:T(8,128)(2,1)S(1)}, bf16[512,1024]{1,0:T(8,128)(2,1)}, u32[]{:S(2)}) copy-start(bf16[512,1024]{1,0:T(8,128)(2,1)} %param.9) | copy-start | bytes 3145732
  7.2 27.4 %copy-start.4 = (bf16[128,1024]{1,0:T(8,128)(2,1)S(1)}, bf16[128,1024]{1,0:T(8,128)(2,1)}, u32[]{:S(2)}) copy-start(bf16[128,1024]{1,0:T(8,128)(2,1)} %param.11) | copy-start | bytes 786436
  9.5 22.8 %all-to-all-start = ((s32[64,1,2,48]{3,2,1,0:T(2,128)}), s32[64,1,2,48]{3,2,1,0:T(2,128)S(1)}, u32[]{:S(2)}, u32[]{:S(2)}) async-start(s32[64,1,2,48]{3,2,1,0:T(2,128)} %stack.8), calls=%async_computation.1 | async-start | bytes 131072 | tf_op jit(solution)/shard_map/all_to_all | solution.py:53
  36.6 4.7 %copy-start.5 = (bf16[128,1024]{1,0:T(8,128)(2,1)S(1)}, bf16[128,1024]{1,0:T(8,128)(2,1)}, u32[]{:S(2)}) copy-start(bf16[128,1024]{1,0:T(8,128)(2,1)} %param.12) | copy-start | bytes 786436
  36.6 56.0 %all-to-all-start.2 = ((bf16[64,16,1024]{2,1,0:T(8,128)(2,1)}), bf16[64,16,1024]{2,1,0:T(8,128)(2,1)S(1)}, u32[]{:S(2)}, u32[]{:S(2)}) async-start(bf16[64,16,1024]{2,1,0:T(8,128)(2,1)} %bitcast.11), calls=%async_computation.3 | async-start | bytes 4194304 | tf_op jit(solution)/shard_map/all_to_all | solution.py:79
  92.6 6.7 %copy-start.1 = (bf16[64,16,1024]{2,1,0:T(8,128)(2,1)}, bf16[64,16,1024]{2,1,0:T(8,128)(2,1)S(1)}, u32[]{:S(2)}) copy-start(bf16[64,16,1024]{2,1,0:T(8,128)(2,1)S(1)} %all-to-all-done.2) | copy-start | bytes 6291460
  92.6 6.1 %copy-start.6 = (s32[1,48]{1,0:T(1,128)S(1)}, s32[1,48]{1,0:T(1,128)}, u32[]{:S(2)}) copy-start(s32[1,48]{1,0:T(1,128)} %param.15) | copy-start | bytes 580
  92.6 57.3 %all-to-all-start.1 = ((bf16[64,16,1024]{2,1,0:T(8,128)(2,1)}), bf16[64,16,1024]{2,1,0:T(8,128)(2,1)}, u32[]{:S(2)}, u32[]{:S(2)}) async-start(bf16[64,16,1024]{2,1,0:T(8,128)(2,1)} %bitcast.7), calls=%async_computation.2 | async-start | bytes 4194304 | tf_op jit(solution)/shard_map/all_to_all | solution.py:80
  149.9 3.0 copy-start.3
  171.0 60.8 %all-to-all-start.4 = ((bf16[64,16,1024]{2,1,0:T(8,128)(2,1)}), bf16[64,16,1024]{2,1,0:T(8,128)(2,1)S(1)}, u32[]{:S(2)}, u32[]{:S(2)}) async-start(bf16[64,16,1024]{2,1,0:T(8,128)(2,1)} %bitcast.57), calls=%async_computation.5 | async-start | bytes 4194304 | tf_op jit(solution)/shard_map/all_to_all | solution.py:105
  180.6 111.3 %reduce-scatter.2.cloned.1.call-start = ((), (), s32[]{:S(2)}) async-start(), calls=%async_computation.6 | async-start | bytes 5242880 | tf_op jit(solution)/shard_map/reduce_scatter | solution.py:124
  231.8 57.2 %all-to-all-start.3 = ((bf16[64,16,1024]{2,1,0:T(8,128)(2,1)}), bf16[64,16,1024]{2,1,0:T(8,128)(2,1)}, u32[]{:S(2)}, u32[]{:S(2)}) async-start(bf16[64,16,1024]{2,1,0:T(8,128)(2,1)} %bitcast.58), calls=%async_computation.4 | async-start | bytes 4194304 | tf_op jit(solution)/shard_map/all_to_all | solution.py:102
  239.2 52.8 %copy-start.2 = (bf16[64,16,1024]{2,1,0:T(8,128)(2,1)S(1)}, bf16[64,16,1024]{2,1,0:T(8,128)(2,1)}, u32[]{:S(2)}) copy-start(bf16[64,16,1024]{2,1,0:T(8,128)(2,1)} %copy-done.1) | copy-start | bytes 6291460
Sparse Core Ops, SparseCore 0:
  190.5 48.8 reduce-scatter.1
